TPU v7x, 512 devices: a whole 4x8x8 slice. The times are simulated.
512 devices in a mesh: doc: 16 (over z, core), gram: 32 (over x, y).
Axes of the slice: x: 4, y: 8, z: 8, core: 2. Of those that a mesh axis runs over, the one named last changes fastest.
Arguments:
- w_factor: bfloat16 [24576, 256], P(('doc', 'gram')), may hold values from 0.003 to 0.1
- h_factor: bfloat16 [49152, 256], P(('gram', 'doc')), may hold values from 0.003 to 0.1
- tile_counts: bfloat16 [16, 32, 24, 128, 128], P('doc', 'gram'), may hold values from 0 to 30, as said below
- tile_rows: int32 [16, 32, 24], P('doc', 'gram'), may hold values from 0 to 11, as said below
- tile_cols: int32 [16, 32, 24], P('doc', 'gram'), may hold values from 0 to 11, as said below
- tile_live: int32 [16, 32], P('doc', 'gram'), may hold values from 1 to 24, as said below
Outputs:
- w_next: bfloat16 [24576, 256], P(('doc', 'gram'))
- h_next: bfloat16 [49152, 256], P(('gram', 'doc'))
Inputs may be any that keep to these rules, and one draw needn't show every extreme that they name: `tile_rows`: within one device pair the first tile_live slots name distinct tiles; slots hold positions in every case. `tile_cols`: see tile_rows. `tile_live`: some device pair holds 24 tiles. `tile_counts`: whole numbers.
All inputs are finite; a program needn't handle non-finite values.
Results may differ from a plain program's by a relative error of at most 0.0021.
Values may be sent and summed in bfloat16 or wider, within the bound.
A program may use at most 64 MiB of HBM per device.

v0:
```python
import jax
import jax.numpy as jnp
from jax import lax
from jax.sharding import PartitionSpec as P

GROUP = 8


def group_terms(w_tiles, h_tiles, rows, cols, counts, keep):
    wt = jnp.take(w_tiles, rows, axis=0)
    ht = jnp.take(h_tiles, cols, axis=0)
    model = jnp.einsum("spk,sqk->spq", wt, ht, preferred_element_type=jnp.float32)
    ratio = (counts.astype(jnp.float32) / model * keep[:, None, None]).astype(jnp.bfloat16)
    w_part = jnp.einsum("spq,sqk->spk", ratio, ht, preferred_element_type=jnp.float32)
    h_part = jnp.einsum("spq,spk->sqk", ratio, wt, preferred_element_type=jnp.float32)
    pick_r = (rows[:, None] == jnp.arange(w_tiles.shape[0], dtype=jnp.int32)[None, :]).astype(
        jnp.float32
    )
    pick_c = (cols[:, None] == jnp.arange(h_tiles.shape[0], dtype=jnp.int32)[None, :]).astype(
        jnp.float32
    )
    add_w = jnp.einsum("st,spk->tpk", pick_r, w_part, precision=lax.Precision.HIGHEST)
    add_h = jnp.einsum("st,spk->tpk", pick_c, h_part, precision=lax.Precision.HIGHEST)
    return (add_w, add_h)


def body(w_factor, h_factor, tile_counts, tile_rows, tile_cols, tile_live):
    topics = w_factor.shape[1]
    w_block = lax.all_gather(w_factor, "gram", axis=0, tiled=True)
    h_block = lax.all_gather(h_factor, "doc", axis=0, tiled=True)
    tile_side = tile_counts.shape[3]
    w_tiles = w_block.reshape(-1, tile_side, topics)
    h_tiles = h_block.reshape(-1, tile_side, topics)
    rows = tile_rows[0, 0]
    cols = tile_cols[0, 0]
    counts = tile_counts[0, 0]
    live = tile_live[0, 0]
    slots = rows.shape[0]
    width = GROUP
    start = (jnp.zeros(w_tiles.shape, jnp.float32), jnp.zeros(h_tiles.shape, jnp.float32))
    steps = slots // width
    marks = (jnp.arange(slots, dtype=jnp.int32) < live).astype(jnp.float32)

    def visit(carry, pieces):
        part_rows, part_cols, part_counts, part_keep = pieces
        add_w, add_h = group_terms(w_tiles, h_tiles, part_rows, part_cols, part_counts, part_keep)
        return ((carry[0] + add_w, carry[1] + add_h), None)

    pieces = (
        rows.reshape(steps, width),
        cols.reshape(steps, width),
        counts.reshape(steps, width, tile_side, tile_side),
        marks.reshape(steps, width),
    )
    (w_numer, h_numer), _ = lax.scan(visit, start, pieces)
    flat_w = w_numer.reshape(-1, topics)
    flat_h = h_numer.reshape(-1, topics)
    w_rows = w_factor.shape[0]
    h_rows = h_factor.shape[0]
    summed_w = lax.psum(flat_w, "gram")
    share_w = lax.dynamic_slice_in_dim(summed_w, lax.axis_index("gram") * w_rows, w_rows, 0)
    summed_h = lax.psum(flat_h, "doc")
    share_h = lax.dynamic_slice_in_dim(summed_h, lax.axis_index("doc") * h_rows, h_rows, 0)
    h_sums = jnp.sum(h_factor.astype(jnp.float32), axis=0)
    w_sums = jnp.sum(w_factor.astype(jnp.float32), axis=0)
    w_denom, h_denom = lax.psum((h_sums, w_sums), ("doc", "gram"))
    w_next = (w_factor.astype(jnp.float32) * share_w / w_denom).astype(jnp.bfloat16)
    h_next = (h_factor.astype(jnp.float32) * share_h / h_denom).astype(jnp.bfloat16)
    return (w_next, h_next)


def solution(mesh):
    in_specs = (
        P(("doc", "gram"), None),
        P(("gram", "doc"), None),
        P("doc", "gram", None, None, None),
        P("doc", "gram", None),
        P("doc", "gram", None),
        P("doc", "gram"),
    )
    out_specs = (P(("doc", "gram"), None), P(("gram", "doc"), None))
    return jax.shard_map(body, mesh=mesh, in_specs=in_specs, out_specs=out_specs, check_vma=False)
```

profile of v0, /device:TPU:1, one launch (start us, length us, event | category | flops | bytes accessed | tf_op | source)
XLA Modules:
  0.0 416.6 jit_solution(2480098275050584792)
XLA Ops:
  7.7 1.3 reduce.6
  9.1 40.1 %all_gather.6 = bf16[1536,256]{1,0:T(8,128)(2,1)S(1)} all-gather(bf16[48,256]{1,0:T(8,128)(2,1)} %param.10), channel_id=1, replica_groups=mesh['doc'=16,'gram'=32] {'gram'}, dimensions={0}, use_global_device_ids=true | all-gather | bytes 811008 | tf_op jit(solution)/shard_map/all_gather | solution.py:29
  49.2 1.3 reduce.7
  50.6 39.1 %all_gather.7 = bf16[1536,256]{1,0:T(8,128)(2,1)} all-gather(bf16[96,256]{1,0:T(8,128)(2,1)} %param.11), channel_id=1, replica_groups=mesh['doc'=16,'gram'=32] {'doc'}, dimensions={0}, use_global_device_ids=true | all-gather | bytes 835584 | tf_op jit(solution)/shard_map/all_gather | solution.py:30
  90.3 38.7 %while.13 = (s32[]{:T(128)}, f32[12,128,256]{2,0,1:T(8,128)S(1)}, f32[12,128,256]{2,0,1:T(8,128)}, s32[3,8]{1,0:T(4,128)S(1)}, bf16[3,8,128,128]{3,2,1,0:T(8,128...) while((s32[]{:T(128)}, f32[12,128,256]{2,0,1:T(8,128)S(1)}, ...), condition=%wide.region_1.3_spmd.clone, body=%wide.region_0.2_spmd.clone.sunk | while | flops 279972160 | bytes 40903584 | solution.py:55
  91.2 1.7 gather_fusion.1
  93.0 0.8 copy-done.4
  93.7 1.3 fusion.44
  95.1 1.4 fusion.45
  96.5 2.5 select_add_fusion.4
  99.4 2.5 select_add_fusion.5
  101.9 1.3 copy-done.1
  104.1 1.7 gather_fusion.1
  105.9 0.8 copy-done.4
  106.6 1.3 fusion.44
  108.0 1.4 fusion.45
  109.4 2.5 select_add_fusion.4
  112.3 2.5 select_add_fusion.5
  114.8 1.3 copy-done.1
  117.0 1.7 gather_fusion.1
  119.5 1.3 fusion.44
  120.9 1.4 fusion.45
  122.3 2.5 select_add_fusion.4
  125.2 2.5 select_add_fusion.5
  127.7 1.3 copy-done.1
  129.0 3.7 copy.9
  132.8 2.1 copy.8
  135.0 95.7 %all-reduce = (f32[256]{0:T(256)S(1)}, f32[256]{0:T(256)S(1)}) all-reduce(f32[256]{0:T(256)S(1)} %convert_reduce_fusion, f32[256]{0:T(256)S(1)} %convert_reduce_fusion.1), channel_id=1, replica_groups=mesh['doc'=16,'gram'=32] {'doc','gram'}, use_global_device_ids=true, to_apply=%region_4.6 | all-reduce | flops 512 | bytes 4096 | tf_op jit(solution)/shard_map/psum | solution.py:66
  230.7 15.8 %all-reduce.6.cloned.1.call-done = f32[1536,256]{1,0:T(8,128)} async-done(((f32[1536,256]{1,0:T(8,128)}), f32[1536,256]{1,0:T(8,128)}) %all-reduce.6.cloned.1.call-update) | async-done | bytes 1572880 | tf_op jit(solution)/shard_map/psum | solution.py:62
  246.6 1.5 fusion.19
  248.1 160.2 %all-reduce.4.cloned.1.call-done = f32[1536,256]{1,0:T(8,128)} async-done(((f32[1536,256]{1,0:T(8,128)}), f32[1536,256]{1,0:T(8,128)}) %all-reduce.4.cloned.1.call-update) | async-done | bytes 1572880 | tf_op jit(solution)/shard_map/psum | solution.py:60
  408.3 1.4 fusion.21
  (77 shorter events, 5.3 us)
Async XLA Ops:
  7.2 239.4 %all-reduce.6.cloned.1.call-start = ((), (), s32[]{:S(2)}) async-start(), calls=%async_computation.1 | async-start | bytes 3145728 | tf_op jit(solution)/shard_map/psum | solution.py:62
  90.3 0.9 copy-start.5
  91.0 2.0 copy-start.2
  92.9 0.8 copy-start.4
  96.5 2.5 copy-start.3
  96.5 2.9 copy-start
  99.4 3.8 copy-start.6
  101.9 1.4 copy-start.1
  103.2 0.9 copy-start.5
  103.9 2.0 copy-start.2
  105.8 0.8 copy-start.4
  109.4 2.5 copy-start.3
  109.4 2.9 copy-start
  112.3 3.8 copy-start.6
  114.8 1.4 copy-start.1
  116.1 0.9 copy-start.5
  116.8 2.0 copy-start.2
  118.7 0.8 copy-start.4
  122.3 2.5 copy-start.3
  122.3 2.9 copy-start
  125.2 3.8 copy-start.6
  127.7 1.4 copy-start.1
  132.7 275.6 %all-reduce.4.cloned.1.call-start = ((), (), s32[]{:S(2)}) async-start(), calls=%async_computation | async-start | bytes 3145728 | tf_op jit(solution)/shard_map/psum | solution.py:60
  132.8 2.2 copy-start.8
  132.8 2.2 copy-start.7
Sparse Core Ops, SparseCore 0:
  132.8 113.6 all-reduce.5
  250.0 158.2 all-reduce.3
where the time goes:
time: 421 us; the launch traced here: 417 us
  waiting for transfers between devices  176 us (42%)
  blocking collectives  175 us (42%)
  matrix products  24.2 us (6%)
  local copies, waits for them, and re-layouts  20.4 us (5%)
  between operations  14.8 us (4%)
  other arithmetic  5.76 us (1%)
    psum x1, waiting for transfers between devices, body(): summed_w = lax.psum(flat_w, 'gram')  160 us
    psum x1, blocking collectives, body(): w_denom, h_denom = lax.psum((h_sums, w_sums), ('doc', 'gram'))  95.7 us
    all_gather x1, blocking collectives, body(): w_block = lax.all_gather(w_factor, 'gram', axis=0, tiled=True)  40.1 us
    all_gather x1, blocking collectives, body(): h_block = lax.all_gather(h_factor, 'doc', axis=0, tiled=True)  39.1 us
    psum x1, waiting for transfers between devices, body(): summed_h = lax.psum(flat_h, 'doc')  15.8 us
  transfers between devices with their start and end apart: 2, of which 2 were waited for; matrix products, arithmetic and copies ran while one was open for 1% of the time, Pallas kernels for 0%

commit v1 on v0

v1 whole, which is shorter than its diff:
```python
import functools

import jax
import jax.numpy as jnp
from jax import lax
from jax.experimental import pallas as pl
from jax.experimental.pallas import tpu as pltpu
from jax.sharding import PartitionSpec as P

MESH = pl.DeviceIdType.MESH
NC = 2
SUB = 16
F32 = jnp.float32
BF16 = jnp.bfloat16


def encode(v):
    s = v * v
    return (s * s).astype(BF16)


def decode(code):
    return lax.rsqrt(lax.rsqrt(code.astype(F32)))


def kernel(nx, ny, nz, tr, tc, slots, tile,
           rows_s, cols_s, map_s, w_ref, h_ref, counts_hbm, wo_ref, ho_ref,
           wbuf, hbuf, counts, rat, rat_t, wfull, wp, hfull, hp,
           wa_in, wa_mid, wa_in2, wb_in, wb_mid, wb_in2, hc_in, hz_mid, hz_in,
           cs_out, cs_x_in, cs_mid, cs_y_in, cd_out, cd_c_in, cd_mid, cd_z_in,
           loc_sem, ss, rs):
    doc = lax.axis_index("doc")
    gram = lax.axis_index("gram")
    z, c = doc // NC, lax.rem(doc, NC)
    x, y = gram // ny, lax.rem(gram, ny)
    jw = wbuf.shape[1] // ny
    ja = jw - 1
    jh = hbuf.shape[0] // (nz * NC)
    gpt = tile // SUB
    topics = w_ref.shape[-1]

    count = [0]

    def rcopy(src, dst, to_doc, to_gram):
        i = count[0]
        count[0] += 1
        return pltpu.make_async_remote_copy(
            src_ref=src, dst_ref=dst, send_sem=ss.at[i], recv_sem=rs.at[i],
            device_id=(to_doc, to_gram), device_id_type=MESH)

    def at_x(k):
        return lax.rem(x + k, nx)

    def at_y(k):
        return lax.rem(y + k, ny)

    def at_z(k):
        return lax.rem(z + k, nz)

    def far_first(n):
        return sorted(range(1, n), key=lambda k: -min(k, n - k))

    partner = z * NC + (1 - c)

    counts_copy = pltpu.make_async_copy(counts_hbm, counts, loc_sem)
    counts_copy.start()
    wbuf[x, pl.ds(y * jw, jw)] = w_ref[...]
    hbuf[pl.ds(doc * jh, jh)] = h_ref[...]

    barrier = pltpu.get_barrier_semaphore()
    peers = 0
    for k in range(1, nx):
        pl.semaphore_signal(barrier, inc=1, device_id=(doc, at_x(k) * ny + y), device_id_type=MESH)
        peers += 1
    for k in range(1, ny):
        pl.semaphore_signal(barrier, inc=1, device_id=(doc, x * ny + at_y(k)), device_id_type=MESH)
        peers += 1
    for k in range(1, nz):
        pl.semaphore_signal(barrier, inc=1, device_id=(at_z(k) * NC + c, gram), device_id_type=MESH)
        peers += 1
    pl.semaphore_signal(barrier, inc=1, device_id=(partner, gram), device_id_type=MESH)
    peers += 1
    rat[slots] = jnp.zeros((tile, tile), BF16)
    rat_t[slots] = jnp.zeros((tile, tile), BF16)
    pl.semaphore_wait(barrier, peers)

    ag_hz = []
    for k in far_first(nz):
        cp = rcopy(h_ref, hbuf.at[pl.ds(doc * jh, jh)], at_z(k) * NC + c, gram)
        cp.start()
        ag_hz.append((k, cp))
    ag_ay = []
    for k in far_first(ny):
        cp = rcopy(w_ref.at[pl.ds(0, ja)], wbuf.at[x, pl.ds(y * jw, ja)], doc, x * ny + at_y(k))
        cp.start()
        ag_ay.append(cp)
    ag_bx = []
    for k in far_first(nx):
        cp = rcopy(w_ref.at[pl.ds(ja, 1)], wbuf.at[x, pl.ds(y * jw + ja, 1)], doc, at_x(k) * ny + y)
        cp.start()
        ag_bx.append(cp)
    ag_hc = [rcopy(h_ref, hbuf.at[pl.ds(doc * jh, jh)], partner, gram)]
    ag_hc[0].start()
    for cp in ag_bx:
        cp.wait_recv()
    ag_by = []
    for k in far_first(ny):
        piece = wbuf.at[:, pl.ds(y * jw + ja, 1)]
        cp = rcopy(piece, piece, doc, x * ny + at_y(k))
        cp.start()
        ag_by.append(cp)
    for cp in ag_ay:
        cp.wait_recv()
    ag_ax = []
    for k in far_first(nx):
        per_y = []
        for yy in range(ny):
            piece = wbuf.at[x, pl.ds(yy * jw, ja)]
            cp = rcopy(piece, piece, doc, at_x(k) * ny + y)
            cp.start()
            per_y.append(cp)
        ag_ax.append(per_y)
    for k, cp in reversed(ag_hz):
        cp.wait_recv()
        came = lax.rem(z + nz - k, nz) * NC + c
        piece = hbuf.at[pl.ds(came * jh, jh)]
        fw = rcopy(piece, piece, partner, gram)
        fw.start()
        ag_hc.append(fw)
    for cp in ag_hc:
        cp.wait_recv()
    for per_y in ag_ax:
        for cp in per_y:
            cp.wait_recv()
    for cp in ag_by:
        cp.wait_recv()

    ones = jnp.ones((8, tile), BF16)

    def w_tile(r):
        per = (ny * jw) // gpt
        return wbuf[r // per, pl.ds(lax.rem(r, per) * gpt, gpt)].reshape(tile, topics)

    def h_tile(q):
        return hbuf[pl.ds(q * gpt, gpt)].reshape(tile, topics)

    sum_h = jnp.zeros((8, topics), F32)
    for q in range(tc):
        sum_h += jnp.dot(ones, h_tile(q), preferred_element_type=F32)
    cs_out[...] = sum_h
    sum_w = jnp.zeros((8, topics), F32)
    for r in range(tr):
        sum_w += jnp.dot(ones, w_tile(r), preferred_element_type=F32)
    cd_out[...] = sum_w

    counts_copy.wait()

    def ratio_step(i, carry):
        for u in range(4):
            s = i * 4 + u
            wt = w_tile(rows_s[s])
            ht = h_tile(cols_s[s])
            model = lax.dot_general(wt, ht, (((1,), (1,)), ((), ())), preferred_element_type=F32)
            ratio = counts[s].astype(F32) / model
            rat[s] = ratio.astype(BF16)
            rat_t[s] = ratio.T.astype(BF16)
        return carry

    lax.fori_loop(0, slots // 4, ratio_step, 0)

    cs_x = []
    for k in range(1, nx):
        cp = rcopy(cs_out, cs_x_in.at[k - 1], doc, at_x(k) * ny + y)
        cp.start()
        cs_x.append(cp)
    cd_c = rcopy(cd_out, cd_c_in, partner, gram)
    cd_c.start()

    wg = tr // nx
    zg = max(1, nz // 4)
    hg = tc * zg // nz
    h_all = hbuf[...].reshape(tc * tile, topics)
    rs_ax = []
    for k in range(1, nx + 1):
        xx = at_x(k)
        lhs = jnp.concatenate([
            jnp.concatenate([rat[map_s[(xx * wg + i) * tc + q]] for q in range(tc)], axis=1)
            for i in range(wg)], axis=0)
        out = jnp.dot(lhs, hbuf[...].reshape(tc * tile, topics), preferred_element_type=F32)
        out = out.reshape(ny * jw, SUB, topics)
        wfull[xx] = out
        wp[xx] = encode(out)
        if k < nx:
            per_y = []
            for yy in range(ny):
                cp = rcopy(wp.at[xx, pl.ds(yy * jw, ja)], wa_in.at[k - 1, pl.ds(yy * ja, ja)],
                           doc, xx * ny + y)
                cp.start()
                per_y.append(cp)
            rs_ax.append(per_y)
    rs_by = []
    for k in far_first(ny):
        yy = at_y(k)
        cp = rcopy(wp.at[:, pl.ds(yy * jw + ja, 1)], wb_in.at[k - 1], doc, x * ny + yy)
        cp.start()
        rs_by.append(cp)
    rs_hc = []
    for k in range(1, nz // zg + 1):
        qq = lax.rem(z // zg + k, nz // zg)
        lhs = jnp.concatenate([
            jnp.concatenate([rat_t[map_s[r * tc + qq * hg + i]] for r in range(tr)], axis=1)
            for i in range(hg)], axis=0)
        out = jnp.dot(lhs, wbuf[...].reshape(tr * tile, topics), preferred_element_type=F32)
        out = out.reshape(hg * gpt, SUB, topics)
        hfull[pl.ds(qq * hg * gpt, hg * gpt)] = out
        hp[pl.ds(qq * hg * gpt, hg * gpt)] = encode(out)
        for i in range(zg):
            zz = qq * zg + i
            cp = rcopy(hp.at[pl.ds((zz * NC + 1 - c) * jh, jh)], hc_in.at[zz], partner, gram)
            cp.start()
            rs_hc.append((zz, cp))

    for per_y in rs_ax:
        for cp in per_y:
            cp.wait_recv()
    rs_ay = []
    for yy in range(ny):
        total = wfull[x, pl.ds(yy * jw, ja)]
        for k in range(nx - 1):
            total += decode(wa_in[k, pl.ds(yy * ja, ja)])
        wfull[x, pl.ds(yy * jw, ja)] = total
        wa_mid[yy] = encode(total)
    for k in far_first(ny):
        yy = at_y(k)
        cp = rcopy(wa_mid.at[yy], wa_in2.at[k - 1], doc, x * ny + yy)
        cp.start()
        rs_ay.append(cp)
    rs_hz = []
    for zz, cp in rs_hc:
        cp.wait_recv()
    for k in far_first(nz):
        zz = at_z(k)
        total = hfull[pl.ds((zz * NC + c) * jh, jh)] + decode(hc_in[zz])
        hz_mid[k - 1] = encode(total)
        cp = rcopy(hz_mid.at[k - 1], hz_in.at[k - 1], zz * NC + c, gram)
        cp.start()
        rs_hz.append((k, cp))
    for cp in rs_by:
        cp.wait_recv()
    total_b = wfull[:, pl.ds(y * jw + ja, 1)]
    for k in range(ny - 1):
        total_b += decode(wb_in[k])
    wfull[:, pl.ds(y * jw + ja, 1)] = total_b
    wb_mid[...] = encode(total_b)
    rs_bx = []
    for k in far_first(nx):
        xx = at_x(k)
        cp = rcopy(wb_mid.at[xx], wb_in2.at[k - 1], doc, xx * ny + y)
        cp.start()
        rs_bx.append(cp)
    for cp in cs_x:
        cp.wait_recv()
    part = cs_out[...]
    for k in range(nx - 1):
        part += cs_x_in[k]
    cs_mid[...] = part
    cs_y = []
    for k in range(1, ny):
        cp = rcopy(cs_mid, cs_y_in.at[k - 1], doc, x * ny + at_y(k))
        cp.start()
        cs_y.append(cp)
    cd_c.wait_recv()
    cd_mid[...] = cd_out[...] + cd_c_in[...]
    cd_z = []
    for k in range(1, nz):
        cp = rcopy(cd_mid, cd_z_in.at[k - 1], at_z(k) * NC + c, gram)
        cp.start()
        cd_z.append(cp)

    own_h = hfull[pl.ds(doc * jh, jh)] + decode(hc_in[z])
    for k, cp in rs_hz:
        cp.wait_recv()
    for k in range(nz - 1):
        own_h += decode(hz_in[k])
    for cp in cd_z:
        cp.wait_recv()
    h_den = cd_mid[...]
    for k in range(nz - 1):
        h_den += cd_z_in[k]
    ho_ref[...] = (h_ref[...].astype(F32) * own_h / h_den[0:1].reshape(1, 1, topics)).astype(BF16)

    for cp in cs_y:
        cp.wait_recv()
    w_den = cs_mid[...]
    for k in range(ny - 1):
        w_den += cs_y_in[k]
    w_den = w_den[0:1].reshape(1, 1, topics)
    for cp in rs_ay:
        cp.wait_recv()
    own_a = wfull[x, pl.ds(y * jw, ja)]
    for k in range(ny - 1):
        own_a += decode(wa_in2[k])
    wo_ref[pl.ds(0, ja)] = (w_ref[pl.ds(0, ja)].astype(F32) * own_a / w_den).astype(BF16)
    for cp in rs_bx:
        cp.wait_recv()
    own_b = wfull[x, pl.ds(y * jw + ja, 1)]
    for k in range(nx - 1):
        own_b += decode(wb_in2[k])
    wo_ref[pl.ds(ja, 1)] = (w_ref[pl.ds(ja, 1)].astype(F32) * own_b / w_den).astype(BF16)

    sends = [cp for _, cp in ag_hz] + ag_ay + ag_bx + ag_hc + ag_by + sum(ag_ax, [])
    sends += cs_x + [cd_c] + sum(rs_ax, []) + rs_by + [cp for _, cp in rs_hc] + rs_ay
    sends += [cp for _, cp in rs_hz] + rs_bx + cs_y + cd_z
    for cp in sends:
        cp.wait_send()


def copies(nx, ny, nz):
    gather = (nz - 1) + (ny - 1) + (nx - 1) + nz + (ny - 1) + (nx - 1) * ny
    scatter = (nx - 1) * ny + (ny - 1) + nz + (ny - 1) + (nz - 1) + (nx - 1)
    sums = (nx - 1) + 1 + (ny - 1) + (nz - 1)
    return gather + scatter + sums


def body(nx, ny, nz, w_factor, h_factor, tile_counts, tile_rows, tile_cols, tile_live):
    topics = w_factor.shape[1]
    slots, tile = tile_counts.shape[2], tile_counts.shape[3]
    tr = w_factor.shape[0] * nx * ny // tile
    tc = h_factor.shape[0] * nz * NC // tile
    rows, cols, live = tile_rows[0, 0], tile_cols[0, 0], tile_live[0, 0]
    jw, jh = w_factor.shape[0] // SUB, h_factor.shape[0] // SUB
    ja = jw - 1
    order = jnp.arange(slots, dtype=jnp.int32)
    hit = (rows * tc + cols)[None, :] == jnp.arange(tr * tc, dtype=jnp.int32)[:, None]
    hit = hit & (order < live)[None, :]
    place = jnp.min(jnp.where(hit, order[None, :], slots), axis=1)

    vmem = pl.BlockSpec(memory_space=pltpu.VMEM)
    smem = pl.BlockSpec(memory_space=pltpu.SMEM)
    n = copies(nx, ny, nz)
    V = pltpu.VMEM
    w_next, h_next = pl.pallas_call(
        functools.partial(kernel, nx, ny, nz, tr, tc, slots, tile),
        out_shape=(jax.ShapeDtypeStruct((jw, SUB, topics), BF16),
                   jax.ShapeDtypeStruct((jh, SUB, topics), BF16)),
        in_specs=[smem, smem, smem, vmem, vmem, pl.BlockSpec(memory_space=pl.ANY)],
        out_specs=(vmem, vmem),
        scratch_shapes=[
            V((nx, ny * jw, SUB, topics), BF16),
            V((nz * NC * jh, SUB, topics), BF16),
            V((slots, tile, tile), BF16),
            V((slots + 1, tile, tile), BF16),
            V((slots + 1, tile, tile), BF16),
            V((nx, ny * jw, SUB, topics), F32),
            V((nx, ny * jw, SUB, topics), BF16),
            V((nz * NC * jh, SUB, topics), F32),
            V((nz * NC * jh, SUB, topics), BF16),
            V((nx - 1, ny * ja, SUB, topics), BF16),
            V((ny, ja, SUB, topics), BF16),
            V((ny - 1, ja, SUB, topics), BF16),
            V((ny - 1, nx, 1, SUB, topics), BF16),
            V((nx, 1, SUB, topics), BF16),
            V((nx - 1, 1, SUB, topics), BF16),
            V((nz, jh, SUB, topics), BF16),
            V((nz - 1, jh, SUB, topics), BF16),
            V((nz - 1, jh, SUB, topics), BF16),
            V((8, topics), F32),
            V((nx - 1, 8, topics), F32),
            V((8, topics), F32),
            V((ny - 1, 8, topics), F32),
            V((8, topics), F32),
            V((8, topics), F32),
            V((8, topics), F32),
            V((nz - 1, 8, topics), F32),
            pltpu.SemaphoreType.DMA(()),
            pltpu.SemaphoreType.DMA((n,)),
            pltpu.SemaphoreType.DMA((n,)),
        ],
        compiler_params=pltpu.CompilerParams(
            collective_id=0, has_side_effects=True, vmem_limit_bytes=56 << 20),
        name="update",
    )(rows, cols, place, w_factor.reshape(jw, SUB, topics), h_factor.reshape(jh, SUB, topics),
      tile_counts.reshape(slots, tile, tile))
    return w_next.reshape(w_factor.shape), h_next.reshape(h_factor.shape)


def solution(mesh, nx=4, nz=8):
    ny = mesh.shape["gram"] // nx
    in_specs = (
        P(("doc", "gram"), None),
        P(("gram", "doc"), None),
        P("doc", "gram", None, None, None),
        P("doc", "gram", None),
        P("doc", "gram", None),
        P("doc", "gram"),
    )
    out_specs = (P(("doc", "gram"), None), P(("gram", "doc"), None))
    return jax.shard_map(functools.partial(body, nx, ny, nz), mesh=mesh, in_specs=in_specs,
                         out_specs=out_specs, check_vma=False)
```

time: 421 us -> 59.5 us (0.14)
  waiting for transfers between devices: 176 us -> 0 us
  blocking collectives: 175 us -> 0 us
  Pallas kernels: 0 us -> 54 us
  matrix products: 24.2 us -> 0 us
  local copies, waits for them, and re-layouts: 20.4 us -> 2.64 us
  between operations: 14.8 us -> 1.32 us
  other arithmetic: 5.76 us -> 0.67 us
    psum x2 -> x0, waiting for transfers between devices: 176 us -> none  [the longest x1 160 us: body(): summed_w = lax.psum(flat_w, 'gram')]
    psum x1 -> x0, blocking collectives: 95.7 us -> none  [body(): w_denom, h_denom = lax.psum((h_sums, w_sums), ('doc', 'gram'))]
    all_gather x2 -> x0, blocking collectives: 79.1 us -> none  [the longest x1 40.1 us: body(): w_block = lax.all_gather(w_factor, 'gram', axis=0, tiled=True)]
    pallas_call x0 -> x1, Pallas kernels: none -> 54 us  [body(): pl.pallas_call(functools.partial(kernel, nx, ny, nz, tr, tc, slots, tile)...]
    dot_general x15 -> x0, matrix products: 24.2 us -> none  [the longest x3 7.43 us: group_terms(): jnp.einsum('st,spk->tpk', pick_c, h_part, precision=lax.Precision.HIGHEST)]
    while x44 -> x0, local copies, waits for them, and re-layouts: 12.8 us -> none
    gather x6 -> x0, local copies, waits for them, and re-layouts: 6.87 us -> none  [the longest x3 5.13 us: group_terms(): ht = jnp.take(h_tiles, cols, axis=0)]
  transfers between devices with their start and end apart: 2 -> 0, of which waited for: 2 -> 0; matrix products, arithmetic and copies ran while one was open for 1% -> 0% of each run, Pallas kernels for 0% -> 0%
where the time goes in v1:
time: 59.5 us; the launch traced here: 58.6 us
  Pallas kernels  54 us (91%)
  local copies, waits for them, and re-layouts  2.64 us (4%)
  between operations  1.32 us (2%)
  other arithmetic  0.67 us (1%)
    pallas_call x1, Pallas kernels, body(): pl.pallas_call(functools.partial(kernel, nx, ny, nz, tr, tc, slots, tile)...  54 us
    unnamed x8, local copies, waits for them, and re-layouts  2.64 us

profile of v1, /device:TPU:1, one launch (start us, length us, event | category | flops | bytes accessed | tf_op | source)
XLA Modules:
  0.0 58.6 jit_solution(16006270188480548802)
XLA Ops:
  1.3 0.0 copy-start.1
  1.3 0.0 copy-start.2
  1.3 0.6 %copy-done.1 = s32[1,1,24]{2,1,0:T(1,128)S(1)} copy-done((s32[1,1,24]{2,1,0:T(1,128)S(1)}, s32[1,1,24]{2,1,0:T(1,128)}, u32[]{:S(2)}) %copy-start.1) | copy-done | bytes 120
  1.9 0.0 copy-done.2
  2.0 0.7 %select_reduce_fusion.map_s = s32[144]{0:T(256)} fusion(s32[24]{0:T(128)S(1)} %multiply_add_fusion, pred[24]{0:T(512)(128)(4,1)S(1)} %iota_compare_fusion.1), kind=kLoop, calls=%fused_computation | loop fusion | flops 13680 | bytes 696 | tf_op jit(solution)/shard_map/reduce_min | solution.py:336
  2.6 54.0 %update.1 = (bf16[3,16,256]{2,1,0:T(8,128)(2,1)}, bf16[6,16,256]{2,1,0:T(8,128)(2,1)}) custom-call(s32[24]{0:T(128)} %bitcast.16, s32[24]{0:T(128)} %bitcast.17, s32[144]{0:T(256)} %select_reduce_fusion.map_s, bf16[3,16,256]{2,1,0:T(8,128)(2,1)} %bitcast.15, bf16[6,16,256]{2,1,0:T(8,128)(2,1)} %bitcast.13, bf16[24,128,128]{2,1,0:T(8,128)(2,1)} %bitcast.11), custom_call_target="tpu_custom_call" | custom-call | tf_op jit(solution)/shard_map/update/pallas_call | solution.py:342
  56.6 0.0 copy-start
  56.7 1.4 %copy.11 = bf16[48,256]{1,0:T(8,128)(2,1)} copy(bf16[48,256]{1,0:T(8,128)(2,1)} %bitcast.14) | data formatting | bytes 49152
  58.0 0.0 copy-done
  58.0 0.6 %copy.12 = bf16[96,256]{1,0:T(8,128)(2,1)} copy(bf16[96,256]{1,0:T(8,128)(2,1)S(1)} %bitcast.12) | data formatting | bytes 98304
  (2 shorter events, 0.0 us)
Async XLA Ops:
  1.3 0.7 %copy-start.1 = (s32[1,1,24]{2,1,0:T(1,128)S(1)}, s32[1,1,24]{2,1,0:T(1,128)}, u32[]{:S(2)}) copy-start(s32[1,1,24]{2,1,0:T(1,128)} %param.9) | copy-start | bytes 292
  1.3 0.7 %copy-start.2 = (s32[1,1,24]{2,1,0:T(1,128)S(1)}, s32[1,1,24]{2,1,0:T(1,128)}, u32[]{:S(2)}) copy-start(s32[1,1,24]{2,1,0:T(1,128)} %param.10) | copy-start | bytes 292
  56.6 1.4 %copy-start = (bf16[6,16,256]{2,1,0:T(8,128)(2,1)S(1)}, bf16[6,16,256]{2,1,0:T(8,128)(2,1)}, u32[]{:S(2)}) copy-start(bf16[6,16,256]{2,1,0:T(8,128)(2,1)} %get-tuple-element.5) | copy-start | bytes 147460

commit v2 on v0

v2 whole, which is shorter than its diff:
```python
import functools

import jax
import jax.numpy as jnp
from jax import lax
from jax.experimental import pallas as pl
from jax.experimental.pallas import tpu as pltpu
from jax.sharding import PartitionSpec as P

MESH = pl.DeviceIdType.MESH
NX, NY, NZ, NC = 4, 8, 8, 2
SUB = 16
F32 = jnp.float32
BF16 = jnp.bfloat16
NEAR = (1, 7, 2, 6, 3, 5, 4)
FAR = (4, 3, 5, 2, 6, 1, 7)


def encode(v):
    s = v * v
    return (s * s).astype(BF16)


def decode(code):
    return lax.rsqrt(lax.rsqrt(code.astype(F32)))


def kernel(tr, tc, slots, tile,
           rows_s, cols_s, live_s, w_ref, h_ref, counts_hbm, wo_ref, ho_ref,
           wbuf, hbuf, counts, rat, rat_t, wfull, wp, hfull, hp,
           wx_in, wy_mid, wy_in, hc_in, hz_mid, h3_in, h4_in, hz_in,
           cs_out, cs_x_in, cs_mid, cs_y_in, cd_out, cd_c_in, cd_mid, cd_z_in,
           map_v, map_s, loc_sem, map_sem, ss, rs):
    doc = lax.axis_index("doc")
    gram = lax.axis_index("gram")
    z, c = doc // NC, lax.rem(doc, NC)
    x, y = gram // NY, lax.rem(gram, NY)
    jw = wbuf.shape[1] // NY
    jh = hbuf.shape[0] // (NZ * NC)
    hh = jh // 2
    gpt = tile // SUB
    topics = w_ref.shape[-1]
    sent = []

    def send(src, dst, to):
        i = len(sent)
        cp = pltpu.make_async_remote_copy(
            src_ref=src, dst_ref=dst, send_sem=ss.at[i], recv_sem=rs.at[i],
            device_id=to, device_id_type=MESH)
        cp.start()
        sent.append(cp)
        return cp

    def at_x(k):
        return lax.rem(x + NX + k, NX)

    def at_y(k):
        return lax.rem(y + NY + k, NY)

    def at_z(k):
        return lax.rem(z + NZ + k, NZ)

    def to_x(k):
        return doc, at_x(k) * NY + y

    def to_y(k):
        return doc, x * NY + at_y(k)

    def to_z(k):
        return at_z(k) * NC + c, gram

    partner = (z * NC + (1 - c), gram)

    barrier = pltpu.get_barrier_semaphore()
    peers = [to_y(k) for k in FAR] + [to_z(k) for k in FAR] + [to_x(k) for k in (2, 1, 3)] + [partner]
    for peer in peers:
        pl.semaphore_signal(barrier, inc=1, device_id=peer, device_id_type=MESH)
    counts_copy = pltpu.make_async_copy(counts_hbm, counts, loc_sem)
    counts_copy.start()
    wbuf[x, pl.ds(y * jw, jw)] = w_ref[...]
    hbuf[pl.ds(doc * jh, jh)] = h_ref[...]
    pl.semaphore_wait(barrier, len(peers))

    def w_piece(k):
        return wbuf.at[x, pl.ds(at_y(k) * jw, jw)]

    def h_piece(k):
        return hbuf.at[pl.ds((at_z(k) * NC + c) * jh, jh)]

    def h_half(k, i):
        return hbuf.at[pl.ds((at_z(k) * NC + c) * jh + i * hh, hh)]

    gx = [send(w_ref, w_piece(0), to_x(k)) for k in (1, 3, 2)]
    gy = {k: send(w_ref, w_piece(0), to_y(k)) for k in NEAR}
    p2 = send(h_ref, h_piece(0), to_z(2))
    m2 = send(h_ref, h_piece(0), to_z(-2))
    p1 = send(h_ref, h_piece(0), to_z(1))
    m1 = send(h_ref, h_piece(0), to_z(-1))
    gc = [send(h_ref, h_piece(0), partner)]

    at_row = lax.broadcasted_iota(jnp.int32, map_v.shape, 0)
    at_col = lax.broadcasted_iota(jnp.int32, map_v.shape, 1)
    place = jnp.full(map_v.shape, slots, jnp.int32)
    for s in range(slots):
        row = jnp.where(s < live_s[0, 0], rows_s[s], -1)
        place = jnp.where((at_row == row) & (at_col == cols_s[s]), s, place)
    map_v[...] = place
    rat[slots] = jnp.zeros((tile, tile), BF16)
    rat_t[slots] = jnp.zeros((tile, tile), BF16)

    def w_on(ks):
        for k in ks:
            gy[k].wait_recv()
            gx.extend(send(w_piece(-k), w_piece(-k), to_x(j)) for j in (1, 3, 2))

    w_on((1, 7, 2, 6))
    map_copy = pltpu.make_async_copy(map_v, map_s, map_sem)
    map_copy.start()
    p2.wait_recv()
    p3 = send(h_piece(-2), h_piece(-2), to_z(1))
    p4 = send(h_half(-2, 0), h_half(-2, 0), to_z(2))
    m2.wait_recv()
    m3 = send(h_piece(2), h_piece(2), to_z(-1))
    m4 = send(h_half(2, 1), h_half(2, 1), to_z(-2))
    gc += [send(h_piece(-2), h_piece(-2), partner), send(h_piece(2), h_piece(2), partner)]
    w_on((3, 5, 4))
    for k, cp in ((-1, p1), (1, m1), (-3, p3), (3, m3)):
        cp.wait_recv()
        gc.append(send(h_piece(k), h_piece(k), partner))
    p4.wait_recv()
    m4.wait_recv()
    gc.append(send(h_piece(4), h_piece(4), partner))
    counts_copy.wait()
    map_copy.wait()
    for cp in gx + gc:
        cp.wait_recv()

    per = (NY * jw) // gpt

    def w_tile(r):
        return wbuf[r // per, pl.ds(lax.rem(r, per) * gpt, gpt)].reshape(tile, topics)

    def h_tile(q):
        return hbuf[pl.ds(q * gpt, gpt)].reshape(tile, topics)

    def ratio_step(i, carry):
        for u in range(4):
            s = i * 4 + u
            model = lax.dot_general(w_tile(rows_s[s]), h_tile(cols_s[s]), (((1,), (1,)), ((), ())),
                                    preferred_element_type=F32)
            ratio = counts[s].astype(F32) / model
            rat[s] = ratio.astype(BF16)
            rat_t[s] = ratio.T.astype(BF16)
        return carry

    lax.fori_loop(0, slots // 4, ratio_step, 0)

    wg = tr // NX
    zg = NZ // 4
    hg = tc // 4
    rx = {}
    for k in (2, 1, 3, 0):
        xx = at_x(k)
        lhs = jnp.concatenate([
            jnp.concatenate([rat[map_s[xx * wg + i, q]] for q in range(tc)], axis=1)
            for i in range(wg)], axis=0)
        out = jnp.dot(lhs, hbuf[...].reshape(tc * tile, topics), preferred_element_type=F32)
        out = out.reshape(NY * jw, SUB, topics)
        if k == 0:
            wfull[...] = out
        else:
            wp[k - 1] = encode(out)
            for j in FAR + (0,):
                at = pl.ds(at_y(j) * jw, jw)
                rx[j, k] = send(wp.at[k - 1, at], wx_in.at[k - 1, at], to_x(k))
    rc = {}
    for k in (2, 1, 3, 0):
        qq = lax.rem(z // zg + k, 4)
        lhs = jnp.concatenate([
            jnp.concatenate([rat_t[map_s[r, qq * hg + i]] for r in range(tr)], axis=1)
            for i in range(hg)], axis=0)
        out = jnp.dot(lhs, wbuf[...].reshape(tr * tile, topics), preferred_element_type=F32)
        out = out.reshape(hg * gpt, SUB, topics)
        at = pl.ds(qq * hg * gpt, hg * gpt)
        hfull[at] = out
        hp[at] = encode(out)
        zz = qq * zg
        rc[k] = [send(hp.at[pl.ds(((zz + i) * NC + 1 - c) * jh, jh)], hc_in.at[zz + i], partner)
                 for i in range(zg)]

    ones = jnp.ones((8, tile), BF16)
    sum_h = jnp.zeros((8, topics), F32)
    for q in range(tc):
        sum_h += jnp.dot(ones, h_tile(q), preferred_element_type=F32)
    cs_out[...] = sum_h
    cs_x = [send(cs_out, cs_x_in.at[k - 1], to_x(k)) for k in range(1, NX)]
    sum_w = jnp.zeros((8, topics), F32)
    for r in range(tr):
        sum_w += jnp.dot(ones, w_tile(r), preferred_element_type=F32)
    cd_out[...] = sum_w
    cd_c = send(cd_out, cd_c_in, partner)

    for k in (2, 1, 3, 0):
        for cp in rc[k]:
            cp.wait_recv()

    def both(k):
        zz = at_z(k)
        return hfull[pl.ds((zz * NC + c) * jh, jh)] + decode(hc_in[zz])

    hz_mid[0] = encode(both(4))
    q4p = send(hz_mid.at[0, pl.ds(0, hh)], h4_in.at[0], to_z(2))
    q4m = send(hz_mid.at[0, pl.ds(hh, hh)], h4_in.at[1], to_z(-2))
    hz_mid[1] = encode(both(3))
    q3p = send(hz_mid.at[1], h3_in.at[0], to_z(1))
    hz_mid[2] = encode(both(-3))
    q3m = send(hz_mid.at[2], h3_in.at[1], to_z(-1))
    hz_mid[3] = encode(both(1))
    q1p = send(hz_mid.at[3], hz_in.at[0], to_z(1))
    hz_mid[4] = encode(both(-1))
    q1m = send(hz_mid.at[4], hz_in.at[1], to_z(-1))

    ry = []

    def w_sum(ks):
        for j in ks:
            at = pl.ds(at_y(j) * jw, jw)
            for k in (1, 3, 2):
                rx[j, k].wait_recv()
            total = wfull[at]
            for k in range(NX - 1):
                total += decode(wx_in[k, at])
            if j == 0:
                return total
            wy_mid[j - 1] = encode(total)
            ry.append(send(wy_mid.at[j - 1], wy_in.at[j - 1], to_y(j)))

    w_sum((4, 3, 5))
    q3p.wait_recv()
    q4p.wait_recv()
    s2 = both(2) + decode(h3_in[0])
    hz_mid[5, pl.ds(0, hh)] = encode(s2[:hh] + decode(h4_in[0]))
    hz_mid[5, pl.ds(hh, hh)] = encode(s2[hh:])
    q2p = send(hz_mid.at[5], hz_in.at[2], to_z(2))
    q3m.wait_recv()
    q4m.wait_recv()
    s2 = both(-2) + decode(h3_in[1])
    hz_mid[6, pl.ds(0, hh)] = encode(s2[:hh])
    hz_mid[6, pl.ds(hh, hh)] = encode(s2[hh:] + decode(h4_in[1]))
    q2m = send(hz_mid.at[6], hz_in.at[3], to_z(-2))
    w_sum((2, 6, 1, 7))

    for cp in cs_x:
        cp.wait_recv()
    part = cs_out[...]
    for k in range(NX - 1):
        part += cs_x_in[k]
    cs_mid[...] = part
    cs_y = [send(cs_mid, cs_y_in.at[k - 1], to_y(k)) for k in FAR]
    cd_c.wait_recv()
    cd_mid[...] = cd_out[...] + cd_c_in[...]
    cd_z = [send(cd_mid, cd_z_in.at[k - 1], to_z(k)) for k in FAR]

    own_w = w_sum((0,))
    own_h = both(0)
    for cp in cd_z + [q1p, q1m, q2p, q2m]:
        cp.wait_recv()
    den = cd_mid[...]
    for k in range(NZ - 1):
        den += cd_z_in[k]
    for k in range(4):
        own_h += decode(hz_in[k])
    ho_ref[...] = (h_ref[...].astype(F32) * own_h / den[0:1].reshape(1, 1, topics)).astype(BF16)

    for cp in cs_y + ry:
        cp.wait_recv()
    den = cs_mid[...]
    for k in range(NY - 1):
        den += cs_y_in[k]
    for k in range(NY - 1):
        own_w += decode(wy_in[k])
    wo_ref[...] = (w_ref[...].astype(F32) * own_w / den[0:1].reshape(1, 1, topics)).astype(BF16)

    assert len(sent) == COPIES, len(sent)
    for cp in sent:
        cp.wait_send()


COPIES = (3 * 8 + 7) + (8 + 8) + 3 * 8 + 8 + 4 + 8 + 7 + 7 + 7


def body(w_factor, h_factor, tile_counts, tile_rows, tile_cols, tile_live):
    topics = w_factor.shape[1]
    slots, tile = tile_counts.shape[2], tile_counts.shape[3]
    tr = w_factor.shape[0] * NX * NY // tile
    tc = h_factor.shape[0] * NZ * NC // tile
    jw, jh = w_factor.shape[0] // SUB, h_factor.shape[0] // SUB

    vmem = pl.BlockSpec(memory_space=pltpu.VMEM)
    smem = pl.BlockSpec(memory_space=pltpu.SMEM)

    def V(*shape, dtype=BF16):
        return pltpu.VMEM(shape, dtype)

    def rows(*lead, dtype=BF16):
        return V(*lead, SUB, topics, dtype=dtype)

    def line(*lead):
        return V(*lead, 8, topics, dtype=F32)

    w_next, h_next = pl.pallas_call(
        functools.partial(kernel, tr, tc, slots, tile),
        out_shape=(jax.ShapeDtypeStruct((jw, SUB, topics), BF16),
                   jax.ShapeDtypeStruct((jh, SUB, topics), BF16)),
        in_specs=[smem, smem, smem, vmem, vmem, pl.BlockSpec(memory_space=pl.ANY)],
        out_specs=(vmem, vmem),
        scratch_shapes=[
            rows(NX, NY * jw), rows(NZ * NC * jh),
            V(slots, tile, tile), V(slots + 1, tile, tile), V(slots + 1, tile, tile),
            rows(NY * jw, dtype=F32), rows(NX - 1, NY * jw),
            rows(NZ * NC * jh, dtype=F32), rows(NZ * NC * jh),
            rows(NX - 1, NY * jw), rows(NY - 1, jw), rows(NY - 1, jw),
            rows(NZ, jh), rows(7, jh), rows(2, jh), rows(2, jh // 2), rows(4, jh),
            line(), line(NX - 1), line(), line(NY - 1),
            line(), line(), line(), line(NZ - 1),
            V(16, 128, dtype=jnp.int32), pltpu.SMEM((16, 128), jnp.int32),
            pltpu.SemaphoreType.DMA(()), pltpu.SemaphoreType.DMA(()),
            pltpu.SemaphoreType.DMA((COPIES,)), pltpu.SemaphoreType.DMA((COPIES,)),
        ],
        compiler_params=pltpu.CompilerParams(
            collective_id=0, has_side_effects=True, vmem_limit_bytes=56 << 20),
        name="update",
    )(tile_rows.reshape(slots), tile_cols.reshape(slots), tile_live,
      w_factor.reshape(jw, SUB, topics), h_factor.reshape(jh, SUB, topics),
      tile_counts.reshape(slots, tile, tile))
    return w_next.reshape(w_factor.shape), h_next.reshape(h_factor.shape)


def solution(mesh):
    in_specs = (
        P(("doc", "gram"), None),
        P(("gram", "doc"), None),
        P("doc", "gram", None, None, None),
        P("doc", "gram", None),
        P("doc", "gram", None),
        P("doc", "gram"),
    )
    out_specs = (P(("doc", "gram"), None), P(("gram", "doc"), None))
    return jax.shard_map(body, mesh=mesh, in_specs=in_specs, out_specs=out_specs, check_vma=False)
```

time: 421 us -> 54.7 us (0.13)
  waiting for transfers between devices: 176 us -> 0 us
  blocking collectives: 175 us -> 0 us
  Pallas kernels: 0 us -> 51.2 us
  matrix products: 24.2 us -> 0 us
  local copies, waits for them, and re-layouts: 20.4 us -> 1.98 us
  between operations: 14.8 us -> 1.29 us
  other arithmetic: 5.76 us -> 0 us
    psum x2 -> x0, waiting for transfers between devices: 176 us -> none  [the longest x1 160 us: body(): summed_w = lax.psum(flat_w, 'gram')]
    psum x1 -> x0, blocking collectives: 95.7 us -> none  [body(): w_denom, h_denom = lax.psum((h_sums, w_sums), ('doc', 'gram'))]
    all_gather x2 -> x0, blocking collectives: 79.1 us -> none  [the longest x1 40.1 us: body(): w_block = lax.all_gather(w_factor, 'gram', axis=0, tiled=True)]
    pallas_call x0 -> x1, Pallas kernels: none -> 51.2 us  [body(): pl.pallas_call(functools.partial(kernel, tr, tc, slots, tile), out_shape=...]
    dot_general x15 -> x0, matrix products: 24.2 us -> none  [the longest x3 7.43 us: group_terms(): jnp.einsum('st,spk->tpk', pick_c, h_part, precision=lax.Precision.HIGHEST)]
    while x44 -> x0, local copies, waits for them, and re-layouts: 12.8 us -> none
    gather x6 -> x0, local copies, waits for them, and re-layouts: 6.87 us -> none  [the longest x3 5.13 us: group_terms(): ht = jnp.take(h_tiles, cols, axis=0)]
  transfers between devices with their start and end apart: 2 -> 0, of which waited for: 2 -> 0; matrix products, arithmetic and copies ran while one was open for 1% -> 0% of each run, Pallas kernels for 0% -> 0%
where the time goes in v2:
time: 54.7 us; the launch traced here: 54.4 us
  Pallas kernels  51.2 us (94%)
  local copies, waits for them, and re-layouts  1.98 us (4%)
  between operations  1.29 us (2%)
    pallas_call x1, Pallas kernels, body(): pl.pallas_call(functools.partial(kernel, tr, tc, slots, tile), out_shape=...  51.2 us
    unnamed x4, local copies, waits for them, and re-layouts  1.98 us

profile of v2, /device:TPU:1, one launch (start us, length us, event | category | flops | bytes accessed | tf_op | source)
XLA Modules:
  0.0 54.4 jit_solution(15220855351443532854)
XLA Ops:
  1.3 51.2 %update.1 = (bf16[3,16,256]{2,1,0:T(8,128)(2,1)}, bf16[6,16,256]{2,1,0:T(8,128)(2,1)}) custom-call(s32[24]{0:T(128)} %bitcast.12, s32[24]{0:T(128)} %bitcast.13, s32[1,1]{1,0:T(1,128)S(6)} %copy.10.live_s, bf16[3,16,256]{2,1,0:T(8,128)(2,1)} %bitcast.10, bf16[6,16,256]{2,1,0:T(8,128)(2,1)} %bitcast.8, bf16[24,128,128]{2,1,0:T(8,128)(2,1)} %bitcast.7), custom_call_target="tpu_custom_call" | custom-call | tf_op jit(solution)/shard_map/update/pallas_call | solution.py:311
  52.4 0.0 copy-start
  52.4 1.4 %copy.11 = bf16[48,256]{1,0:T(8,128)(2,1)} copy(bf16[48,256]{1,0:T(8,128)(2,1)} %bitcast.11) | data formatting | bytes 49152
  53.8 0.0 copy-done
  53.8 0.6 %copy.12 = bf16[96,256]{1,0:T(8,128)(2,1)} copy(bf16[96,256]{1,0:T(8,128)(2,1)S(1)} %bitcast.9) | data formatting | bytes 98304
Async XLA Ops:
  52.4 1.4 %copy-start = (bf16[6,16,256]{2,1,0:T(8,128)(2,1)S(1)}, bf16[6,16,256]{2,1,0:T(8,128)(2,1)}, u32[]{:S(2)}) copy-start(bf16[6,16,256]{2,1,0:T(8,128)(2,1)} %get-tuple-element.5) | copy-start | bytes 147460

commit v3 on v2

--- a/solution.py
+++ b/solution.py
@@ -26,11 +26,11 @@
 
 
 def kernel(tr, tc, slots, tile,
-           rows_s, cols_s, live_s, w_ref, h_ref, counts_hbm, wo_ref, ho_ref,
+           live_s, rows_hbm, cols_hbm, w_ref, h_ref, counts_hbm, wo_ref, ho_ref,
            wbuf, hbuf, counts, rat, rat_t, wfull, wp, hfull, hp,
            wx_in, wy_mid, wy_in, hc_in, hz_mid, h3_in, h4_in, hz_in,
            cs_out, cs_x_in, cs_mid, cs_y_in, cd_out, cd_c_in, cd_mid, cd_z_in,
-           map_v, map_s, loc_sem, map_sem, ss, rs):
+           rows_s, cols_s, map_v, map_s, loc_sem, ss, rs):
     doc = lax.axis_index("doc")
     gram = lax.axis_index("gram")
     z, c = doc // NC, lax.rem(doc, NC)
@@ -75,10 +75,12 @@
     peers = [to_y(k) for k in FAR] + [to_z(k) for k in FAR] + [to_x(k) for k in (2, 1, 3)] + [partner]
     for peer in peers:
         pl.semaphore_signal(barrier, inc=1, device_id=peer, device_id_type=MESH)
-    counts_copy = pltpu.make_async_copy(counts_hbm, counts, loc_sem)
-    counts_copy.start()
-    wbuf[x, pl.ds(y * jw, jw)] = w_ref[...]
-    hbuf[pl.ds(doc * jh, jh)] = h_ref[...]
+    local = [(rows_hbm, rows_s), (cols_hbm, cols_s),
+             (w_ref, wbuf.at[x, pl.ds(y * jw, jw)]), (h_ref, hbuf.at[pl.ds(doc * jh, jh)]),
+             (counts_hbm, counts)]
+    local = [pltpu.make_async_copy(src, dst, loc_sem.at[i]) for i, (src, dst) in enumerate(local)]
+    for cp in local:
+        cp.start()
     pl.semaphore_wait(barrier, len(peers))
 
     def w_piece(k):
@@ -98,6 +100,8 @@
     m1 = send(h_ref, h_piece(0), to_z(-1))
     gc = [send(h_ref, h_piece(0), partner)]
 
+    for cp in local[:2]:
+        cp.wait()
     at_row = lax.broadcasted_iota(jnp.int32, map_v.shape, 0)
     at_col = lax.broadcasted_iota(jnp.int32, map_v.shape, 1)
     place = jnp.full(map_v.shape, slots, jnp.int32)
@@ -114,7 +118,7 @@
             gx.extend(send(w_piece(-k), w_piece(-k), to_x(j)) for j in (1, 3, 2))
 
     w_on((1, 7, 2, 6))
-    map_copy = pltpu.make_async_copy(map_v, map_s, map_sem)
+    map_copy = pltpu.make_async_copy(map_v, map_s, loc_sem.at[len(local)])
     map_copy.start()
     p2.wait_recv()
     p3 = send(h_piece(-2), h_piece(-2), to_z(1))
@@ -130,10 +134,20 @@
     p4.wait_recv()
     m4.wait_recv()
     gc.append(send(h_piece(4), h_piece(4), partner))
-    counts_copy.wait()
+    for cp in local[2:]:
+        cp.wait()
     map_copy.wait()
-    for cp in gx + gc:
-        cp.wait_recv()
+    def column_sums(buf):
+        return jnp.sum(buf[...].astype(F32).reshape(-1, 8, topics), axis=0)
+
+    for cp in gc:
+        cp.wait_recv()
+    cs_out[...] = column_sums(hbuf)
+    cs_x = [send(cs_out, cs_x_in.at[k - 1], to_x(k)) for k in range(1, NX)]
+    for cp in gx:
+        cp.wait_recv()
+    cd_out[...] = column_sums(wbuf)
+    cd_c = send(cd_out, cd_c_in, partner)
 
     per = (NY * jw) // gpt
 
@@ -144,20 +158,31 @@
         return hbuf[pl.ds(q * gpt, gpt)].reshape(tile, topics)
 
     def ratio_step(i, carry):
-        for u in range(4):
-            s = i * 4 + u
+        for u in range(12):
+            s = i * 12 + u
             model = lax.dot_general(w_tile(rows_s[s]), h_tile(cols_s[s]), (((1,), (1,)), ((), ())),
                                     preferred_element_type=F32)
-            ratio = counts[s].astype(F32) / model
-            rat[s] = ratio.astype(BF16)
-            rat_t[s] = ratio.T.astype(BF16)
+            ratio = (counts[s].astype(F32) / model).astype(BF16)
+            rat[s] = ratio
+            rat_t[s] = ratio.T
         return carry
 
-    lax.fori_loop(0, slots // 4, ratio_step, 0)
+    lax.fori_loop(0, slots // 12, ratio_step, 0)
 
     wg = tr // NX
     zg = NZ // 4
     hg = tc // 4
+    for cp in cs_x:
+        cp.wait_recv()
+    part = cs_out[...]
+    for k in range(NX - 1):
+        part += cs_x_in[k]
+    cs_mid[...] = part
+    cs_y = [send(cs_mid, cs_y_in.at[k - 1], to_y(k)) for k in FAR]
+    cd_c.wait_recv()
+    cd_mid[...] = cd_out[...] + cd_c_in[...]
+    cd_z = [send(cd_mid, cd_z_in.at[k - 1], to_z(k)) for k in FAR]
+
     rx = {}
     for k in (2, 1, 3, 0):
         xx = at_x(k)
@@ -170,9 +195,11 @@
             wfull[...] = out
         else:
             wp[k - 1] = encode(out)
+        if k == 3:
             for j in FAR + (0,):
                 at = pl.ds(at_y(j) * jw, jw)
-                rx[j, k] = send(wp.at[k - 1, at], wx_in.at[k - 1, at], to_x(k))
+                for i in (2, 1, 3):
+                    rx[j, i] = send(wp.at[i - 1, at], wx_in.at[i - 1, at], to_x(i))
     rc = {}
     for k in (2, 1, 3, 0):
         qq = lax.rem(z // zg + k, 4)
@@ -188,17 +215,14 @@
         rc[k] = [send(hp.at[pl.ds(((zz + i) * NC + 1 - c) * jh, jh)], hc_in.at[zz + i], partner)
                  for i in range(zg)]
 
-    ones = jnp.ones((8, tile), BF16)
-    sum_h = jnp.zeros((8, topics), F32)
-    for q in range(tc):
-        sum_h += jnp.dot(ones, h_tile(q), preferred_element_type=F32)
-    cs_out[...] = sum_h
-    cs_x = [send(cs_out, cs_x_in.at[k - 1], to_x(k)) for k in range(1, NX)]
-    sum_w = jnp.zeros((8, topics), F32)
-    for r in range(tr):
-        sum_w += jnp.dot(ones, w_tile(r), preferred_element_type=F32)
-    cd_out[...] = sum_w
-    cd_c = send(cd_out, cd_c_in, partner)
+    left = []
+
+    def drain(cps):
+        for cp in cps:
+            cp.wait_send()
+        left.extend(cps)
+
+    drain(gx + gc + list(gy.values()) + [p1, m1, p2, m2, p3, m3, p4, m4])
 
     for k in (2, 1, 3, 0):
         for cp in rc[k]:
@@ -250,16 +274,7 @@
     q2m = send(hz_mid.at[6], hz_in.at[3], to_z(-2))
     w_sum((2, 6, 1, 7))
 
-    for cp in cs_x:
-        cp.wait_recv()
-    part = cs_out[...]
-    for k in range(NX - 1):
-        part += cs_x_in[k]
-    cs_mid[...] = part
-    cs_y = [send(cs_mid, cs_y_in.at[k - 1], to_y(k)) for k in FAR]
-    cd_c.wait_recv()
-    cd_mid[...] = cd_out[...] + cd_c_in[...]
-    cd_z = [send(cd_mid, cd_z_in.at[k - 1], to_z(k)) for k in FAR]
+    drain(list(rx.values()) + sum(rc.values(), []) + cs_x + [cd_c, q4p, q4m, q3p, q3m])
 
     own_w = w_sum((0,))
     own_h = both(0)
@@ -270,7 +285,7 @@
         den += cd_z_in[k]
     for k in range(4):
         own_h += decode(hz_in[k])
-    ho_ref[...] = (h_ref[...].astype(F32) * own_h / den[0:1].reshape(1, 1, topics)).astype(BF16)
+    ho_ref[...] = (hbuf[pl.ds(doc * jh, jh)].astype(F32) * own_h / jnp.sum(den, axis=0).reshape(1, 1, topics)).astype(BF16)
 
     for cp in cs_y + ry:
         cp.wait_recv()
@@ -279,11 +294,12 @@
         den += cs_y_in[k]
     for k in range(NY - 1):
         own_w += decode(wy_in[k])
-    wo_ref[...] = (w_ref[...].astype(F32) * own_w / den[0:1].reshape(1, 1, topics)).astype(BF16)
+    wo_ref[...] = (wbuf[x, pl.ds(y * jw, jw)].astype(F32) * own_w / jnp.sum(den, axis=0).reshape(1, 1, topics)).astype(BF16)
 
     assert len(sent) == COPIES, len(sent)
     for cp in sent:
-        cp.wait_send()
+        if not any(cp is done for done in left):
+            cp.wait_send()
 
 
 COPIES = (3 * 8 + 7) + (8 + 8) + 3 * 8 + 8 + 4 + 8 + 7 + 7 + 7
@@ -297,7 +313,6 @@
     jw, jh = w_factor.shape[0] // SUB, h_factor.shape[0] // SUB
 
     vmem = pl.BlockSpec(memory_space=pltpu.VMEM)
-    smem = pl.BlockSpec(memory_space=pltpu.SMEM)
 
     def V(*shape, dtype=BF16):
         return pltpu.VMEM(shape, dtype)
@@ -312,7 +327,7 @@
         functools.partial(kernel, tr, tc, slots, tile),
         out_shape=(jax.ShapeDtypeStruct((jw, SUB, topics), BF16),
                    jax.ShapeDtypeStruct((jh, SUB, topics), BF16)),
-        in_specs=[smem, smem, smem, vmem, vmem, pl.BlockSpec(memory_space=pl.ANY)],
+        in_specs=[pl.BlockSpec(memory_space=pltpu.SMEM)] + [pl.BlockSpec(memory_space=pltpu.HBM)] * 5,
         out_specs=(vmem, vmem),
         scratch_shapes=[
             rows(NX, NY * jw), rows(NZ * NC * jh),
@@ -323,16 +338,18 @@
             rows(NZ, jh), rows(7, jh), rows(2, jh), rows(2, jh // 2), rows(4, jh),
             line(), line(NX - 1), line(), line(NY - 1),
             line(), line(), line(), line(NZ - 1),
+            pltpu.SMEM((slots,), jnp.int32), pltpu.SMEM((slots,), jnp.int32),
             V(16, 128, dtype=jnp.int32), pltpu.SMEM((16, 128), jnp.int32),
-            pltpu.SemaphoreType.DMA(()), pltpu.SemaphoreType.DMA(()),
+            pltpu.SemaphoreType.DMA((6,)),
             pltpu.SemaphoreType.DMA((COPIES,)), pltpu.SemaphoreType.DMA((COPIES,)),
         ],
         compiler_params=pltpu.CompilerParams(
-            collective_id=0, has_side_effects=True, vmem_limit_bytes=56 << 20),
+            collective_id=0, has_side_effects=True, vmem_limit_bytes=24 << 20),
         name="update",
-    )(tile_rows.reshape(slots), tile_cols.reshape(slots), tile_live,
-      w_factor.reshape(jw, SUB, topics), h_factor.reshape(jh, SUB, topics),
-      tile_counts.reshape(slots, tile, tile))
+    )(tile_live, *(pltpu.with_memory_space_constraint(a, pltpu.HBM) for a in (
+        tile_rows.reshape(slots), tile_cols.reshape(slots),
+        w_factor.reshape(jw, SUB, topics), h_factor.reshape(jh, SUB, topics),
+        tile_counts.reshape(slots, tile, tile))))
     return w_next.reshape(w_factor.shape), h_next.reshape(h_factor.shape)
 
 

time: 54.7 us -> 48.4 us (0.88)
  Pallas kernels: 51.2 us -> 45.8 us
  local copies, waits for them, and re-layouts: 1.98 us -> 1.23 us
    pallas_call x1, Pallas kernels: 51.2 us -> 45.8 us  [body(): pl.pallas_call(functools.partial(kernel, tr, tc, slots, tile), out_shape=...]
    unnamed x4 -> x2, local copies, waits for them, and re-layouts: 1.98 us -> 1.23 us
where the time goes in v3:
time: 48.4 us; the launch traced here: 48.3 us
  Pallas kernels  45.8 us (95%)
  between operations  1.29 us (3%)
  local copies, waits for them, and re-layouts  1.23 us (3%)
    pallas_call x1, Pallas kernels, body(): pl.pallas_call(functools.partial(kernel, tr, tc, slots, tile), out_shape=...  45.8 us
    unnamed x2, local copies, waits for them, and re-layouts  1.23 us

profile of v3, /device:TPU:1, one launch (start us, length us, event | category | flops | bytes accessed | tf_op | source)
XLA Modules:
  0.0 48.3 jit_solution(5857382038727791212)
XLA Ops:
  1.3 45.8 %update.1 = (bf16[3,16,256]{2,1,0:T(8,128)(2,1)S(1)}, bf16[6,16,256]{2,1,0:T(8,128)(2,1)S(1)}) custom-call(s32[1,1]{1,0:T(1,128)S(6)} %copy.10.live_s, s32[24]{0:T(128)} %bitcast.12, s32[24]{0:T(128)} %bitcast.13, bf16[3,16,256]{2,1,0:T(8,128)(2,1)} %bitcast.11, bf16[6,16,256]{2,1,0:T(8,128)(2,1)} %bitcast.10, bf16[24,128,128]{2,1,0:T(8,128)(2,1)} %bitcast.9), custom_call_target="tpu_custom_call" | custom-call | tf_op jit(solution)/shard_map/update/pallas_call | solution.py:326
  47.1 0.6 %copy.11 = bf16[48,256]{1,0:T(8,128)(2,1)} copy(bf16[48,256]{1,0:T(8,128)(2,1)S(1)} %bitcast.8) | data formatting | bytes 49152
  47.7 0.6 %copy.12 = bf16[96,256]{1,0:T(8,128)(2,1)} copy(bf16[96,256]{1,0:T(8,128)(2,1)S(1)} %bitcast.7) | data formatting | bytes 98304

commit v4 on v3

--- a/solution.py
+++ b/solution.py
@@ -117,7 +117,7 @@
             gy[k].wait_recv()
             gx.extend(send(w_piece(-k), w_piece(-k), to_x(j)) for j in (1, 3, 2))
 
-    w_on((1, 7, 2, 6))
+    w_on((1, 7))
     map_copy = pltpu.make_async_copy(map_v, map_s, loc_sem.at[len(local)])
     map_copy.start()
     p2.wait_recv()
@@ -127,7 +127,7 @@
     m3 = send(h_piece(2), h_piece(2), to_z(-1))
     m4 = send(h_half(2, 1), h_half(2, 1), to_z(-2))
     gc += [send(h_piece(-2), h_piece(-2), partner), send(h_piece(2), h_piece(2), partner)]
-    w_on((3, 5, 4))
+    w_on((2, 6, 3, 5, 4))
     for k, cp in ((-1, p1), (1, m1), (-3, p3), (3, m3)):
         cp.wait_recv()
         gc.append(send(h_piece(k), h_piece(k), partner))
@@ -302,6 +302,14 @@
             cp.wait_send()
 
 
+def place(w_ref, h_ref, wo_ref, ho_ref, sem):
+    copies = [pltpu.make_async_copy(w_ref, wo_ref, sem.at[0]), pltpu.make_async_copy(h_ref, ho_ref, sem.at[1])]
+    for cp in copies:
+        cp.start()
+    for cp in copies:
+        cp.wait()
+
+
 COPIES = (3 * 8 + 7) + (8 + 8) + 3 * 8 + 8 + 4 + 8 + 7 + 7 + 7
 
 
@@ -350,6 +358,17 @@
         tile_rows.reshape(slots), tile_cols.reshape(slots),
         w_factor.reshape(jw, SUB, topics), h_factor.reshape(jh, SUB, topics),
         tile_counts.reshape(slots, tile, tile))))
+    hbm = pl.BlockSpec(memory_space=pl.ANY)
+    w_next, h_next = pl.pallas_call(
+        place,
+        out_shape=(jax.ShapeDtypeStruct((jw, SUB, topics), BF16),
+                   jax.ShapeDtypeStruct((jh, SUB, topics), BF16)),
+        in_specs=[hbm, hbm],
+        out_specs=(pl.BlockSpec(memory_space=pltpu.HBM), pl.BlockSpec(memory_space=pltpu.HBM)),
+        scratch_shapes=[pltpu.SemaphoreType.DMA((2,))],
+        compiler_params=pltpu.CompilerParams(vmem_limit_bytes=1 << 20),
+        name="place",
+    )(w_next, h_next)
     return w_next.reshape(w_factor.shape), h_next.reshape(h_factor.shape)
 
 

time: 48.4 us -> 47.7 us (0.986)
  local copies, waits for them, and re-layouts: 1.23 us -> 0 us
  Pallas kernels: 45.8 us -> 46.3 us
    unnamed x2 -> x0, local copies, waits for them, and re-layouts: 1.23 us -> none
    pallas_call x0 -> x1, Pallas kernels: none -> 0.65 us  [body(): pl.pallas_call(place, out_shape=(jax.ShapeDtypeStruct((jw, SUB, topics),...]
where the time goes in v4:
time: 47.7 us; the launch traced here: 47.6 us
  Pallas kernels  46.3 us (97%)
  between operations  1.29 us (3%)
    pallas_call x1, Pallas kernels, body(): pl.pallas_call(functools.partial(kernel, tr, tc, slots, tile), out_shape=...  45.7 us

profile of v4, /device:TPU:1, one launch (start us, length us, event | category | flops | bytes accessed | tf_op | source)
XLA Modules:
  0.0 47.6 jit_solution(4148944087714427428)
XLA Ops:
  1.3 45.7 %update.1 = (bf16[3,16,256]{2,1,0:T(8,128)(2,1)S(1)}, bf16[6,16,256]{2,1,0:T(8,128)(2,1)S(1)}) custom-call(s32[1,1]{1,0:T(1,128)S(6)} %copy.8.live_s, s32[24]{0:T(128)} %bitcast.10, s32[24]{0:T(128)} %bitcast.11, bf16[3,16,256]{2,1,0:T(8,128)(2,1)} %bitcast.9, bf16[6,16,256]{2,1,0:T(8,128)(2,1)} %bitcast.8, bf16[24,128,128]{2,1,0:T(8,128)(2,1)} %bitcast.7), custom_call_target="tpu_custom_call" | custom-call | tf_op jit(solution)/shard_map/update/pallas_call | solution.py:334
  47.0 0.6 %place.1 = (bf16[3,16,256]{2,1,0:T(8,128)(2,1)}, bf16[6,16,256]{2,1,0:T(8,128)(2,1)}) custom-call(bf16[3,16,256]{2,1,0:T(8,128)(2,1)S(1)} %get-tuple-element.6.w_ref, bf16[6,16,256]{2,1,0:T(8,128)(2,1)S(1)} %get-tuple-element.7.h_ref), custom_call_target="tpu_custom_call" | custom-call | tf_op jit(solution)/shard_map/place/pallas_call | solution.py:362

commit v5 on v4

--- a/solution.py
+++ b/solution.py
@@ -127,10 +127,15 @@
     m3 = send(h_piece(2), h_piece(2), to_z(-1))
     m4 = send(h_half(2, 1), h_half(2, 1), to_z(-2))
     gc += [send(h_piece(-2), h_piece(-2), partner), send(h_piece(2), h_piece(2), partner)]
-    w_on((2, 6, 3, 5, 4))
-    for k, cp in ((-1, p1), (1, m1), (-3, p3), (3, m3)):
+    w_on((2, 6))
+    for k, cp in ((-1, p1), (1, m1)):
         cp.wait_recv()
         gc.append(send(h_piece(k), h_piece(k), partner))
+    w_on((3, 5))
+    for k, cp in ((-3, p3), (3, m3)):
+        cp.wait_recv()
+        gc.append(send(h_piece(k), h_piece(k), partner))
+    w_on((4,))
     p4.wait_recv()
     m4.wait_recv()
     gc.append(send(h_piece(4), h_piece(4), partner))

time: 47.7 us -> 47.8 us (level)
  no operation moved by 1% of the time
where the time goes in v5:
time: 47.8 us; the launch traced here: 47.6 us
  Pallas kernels  46.4 us (97%)
  between operations  1.29 us (3%)
    pallas_call x1, Pallas kernels, body(): pl.pallas_call(functools.partial(kernel, tr, tc, slots, tile), out_shape=...  45.7 us

profile of v5, /device:TPU:1, one launch (start us, length us, event | category | flops | bytes accessed | tf_op | source)
XLA Modules:
  0.0 47.6 jit_solution(331292118513201527)
XLA Ops:
  1.3 45.7 %update.1 = (bf16[3,16,256]{2,1,0:T(8,128)(2,1)S(1)}, bf16[6,16,256]{2,1,0:T(8,128)(2,1)S(1)}) custom-call(s32[1,1]{1,0:T(1,128)S(6)} %copy.8.live_s, s32[24]{0:T(128)} %bitcast.10, s32[24]{0:T(128)} %bitcast.11, bf16[3,16,256]{2,1,0:T(8,128)(2,1)} %bitcast.9, bf16[6,16,256]{2,1,0:T(8,128)(2,1)} %bitcast.8, bf16[24,128,128]{2,1,0:T(8,128)(2,1)} %bitcast.7), custom_call_target="tpu_custom_call" | custom-call | tf_op jit(solution)/shard_map/update/pallas_call | solution.py:339
  47.0 0.6 %place.1 = (bf16[3,16,256]{2,1,0:T(8,128)(2,1)}, bf16[6,16,256]{2,1,0:T(8,128)(2,1)}) custom-call(bf16[3,16,256]{2,1,0:T(8,128)(2,1)S(1)} %get-tuple-element.6.w_ref, bf16[6,16,256]{2,1,0:T(8,128)(2,1)S(1)} %get-tuple-element.7.h_ref), custom_call_target="tpu_custom_call" | custom-call | tf_op jit(solution)/shard_map/place/pallas_call | solution.py:367
